TPU v7x, 32 devices: a whole 2x2x4 slice. The times are simulated.
32 devices in a mesh: sec: 4 (over y, core), grp: 8 (over z, x).
Axes of the slice: x: 2, y: 2, z: 4, core: 2. Of those that a mesh axis runs over, the one named last changes fastest.
Arguments:
- solution_in: float32 [2, 32, 4, 6144], P(None, 'grp', None, 'sec'), may hold values from -6 to 6
- residual_in: float32 [2, 32, 4, 6144], P(None, 'grp', None, 'sec'), may hold values from -6 to 6
- direction_in: float32 [2, 32, 4, 6144], P(None, 'grp', None, 'sec'), may hold values from -6 to 6
- legendre: bfloat16 [32, 2, 128, 6144], P('grp', None, None, 'sec'), may hold values from -0.0034179688 to 0.0034179688
- inverse_prior: float32 [2, 6144], P(None, 'sec'), may hold values from 0.3 to 10
- noise_qq: float32 [128, 8192], P('grp', 'sec'), may hold values from 0.5 to 4
- noise_qu: float32 [128, 8192], P('grp', 'sec'), may hold values from -0.3 to 0.3
- noise_uu: float32 [128, 8192], P('grp', 'sec'), may hold values from 0.5 to 4
- pixel_mask: int32 [128, 8192], P('grp', 'sec'), may hold values 0 or 1
- cycle_phase: float32 [128], replicated, as said below
- m_values: int32 [32], replicated, may hold values from 0 to 6143, as said below
Outputs:
- solution: float32 [2, 32, 4, 6144], P(None, 'grp', None, 'sec')
- residual: float32 [2, 32, 4, 6144], P(None, 'grp', None, 'sec')
- direction: float32 [2, 32, 4, 6144], P(None, 'grp', None, 'sec')
Inputs may be any that keep to these rules, and one draw needn't show every extreme that they name: `m_values`: the slots' m values are distinct, and exactly one slot has m = 0. `cycle_phase`: each phase lies between 0 and 2 pi / 8192.
All inputs are finite; a program needn't handle non-finite values. No bound on the sum of `pixel_mask` on one device may be relied on, other than what follows from the above.
Results may differ from a plain program's by a relative error of at most 0.025.
Values sent between devices are 32-bit elements; how exact they have to be, the bound alone decides.
No kernel may reach another device: no remote copies, remote signals or barrier semaphores. Data moves between devices by JAX's collectives and lax.ppermute only.
A program may use at most 64 MiB of HBM per device.

v0:
```python
import math
import jax
import jax.numpy as jnp
from jax import lax
from jax.sharding import PartitionSpec as P

ITERS = 4
full_turn = 2.0 * math.pi


def combine_modes(prod):
    plus = prod[:, :, 0]
    minus = prod[:, :, 1]
    return jnp.stack(
        [
            -plus[:, :, 0] + minus[:, :, 3],
            -plus[:, :, 1] - minus[:, :, 2],
            -plus[:, :, 2] - minus[:, :, 1],
            -plus[:, :, 3] + minus[:, :, 0],
        ],
        axis=2,
    )


def adjoint_terms(field):
    half = field.astype(jnp.bfloat16)
    minus_part = jnp.stack([half[:, :, 3], -half[:, :, 2], -half[:, :, 1], half[:, :, 0]], axis=2)
    return jnp.stack([-half, minus_part], axis=2)


def legendre_forward(coeffs, legendre):
    half = coeffs.astype(jnp.bfloat16)
    prod = jnp.einsum("msrl,bmcl->bmscr", legendre, half, preferred_element_type=jnp.float32)
    return combine_modes(prod)


def legendre_adjoint(field, legendre):
    both = adjoint_terms(field)
    return jnp.einsum("msrl,bmscr->bmcl", legendre, both, preferred_element_type=jnp.float32)


def phi_table(m_values, start, count, total):
    index = start + jnp.arange(count, dtype=jnp.int32)
    folded = m_values[:, None] * index[None, :] % total
    angle = folded.astype(jnp.float32) * (full_turn / total)
    weight = jnp.where(m_values == 0, 1.0, 2.0).astype(jnp.float32)[:, None]
    return jnp.concatenate([weight * jnp.cos(angle), -weight * jnp.sin(angle)], axis=0)


def pixel_segment(field, cosines, sine_table, table, noise_qq, noise_qu, noise_uu, mask_f):
    count = field.shape[0]
    modes = field.shape[1]
    cycles = field.shape[3]
    parts = field.reshape(count, modes, 2, 2, cycles)
    real = parts[:, :, :, 0]
    imag = parts[:, :, :, 1]
    cosm = cosines[None, :, None, :]
    sinm = sine_table[None, :, None, :]
    rot_re = real * cosm - imag * sinm
    rot_im = real * sinm + imag * cosm
    rows = (
        jnp.stack([rot_re, rot_im], axis=1)
        .transpose(0, 3, 4, 1, 2)
        .reshape(count * 2 * cycles, 2 * modes)
    )
    pixels = jnp.dot(
        rows, table, precision=lax.Precision.HIGHEST, preferred_element_type=jnp.float32
    )
    pixels = pixels.reshape(count, 2, cycles, -1)
    qpart = pixels[:, 0]
    upart = pixels[:, 1]
    wq = mask_f * (noise_qq * qpart + noise_qu * upart)
    wu = mask_f * (noise_qu * qpart + noise_uu * upart)
    weighted = jnp.stack([wq, wu], axis=1).reshape(count * 2 * cycles, -1)
    back = jnp.dot(
        weighted, table.T, precision=lax.Precision.HIGHEST, preferred_element_type=jnp.float32
    )
    back = back.reshape(count, 2, cycles, 2, modes)
    out = jnp.stack([back[:, :, :, 0], back[:, :, :, 1]], axis=2)
    return out.transpose(0, 4, 1, 2, 3).reshape(count, modes, 4, cycles)


def rotate_back(field, cosines, sine_table):
    count = field.shape[0]
    modes = field.shape[1]
    cycles = field.shape[3]
    parts = field.reshape(count, modes, 2, 2, cycles)
    real = parts[:, :, :, 0]
    imag = parts[:, :, :, 1]
    cosm = cosines[None, :, None, :]
    sinm = sine_table[None, :, None, :]
    turned_real = real * cosm + imag * sinm
    turned_imag = imag * cosm - real * sinm
    return jnp.stack([turned_real, turned_imag], axis=3).reshape(count, modes, 4, cycles)


def totals(values):
    return jnp.sum(values, axis=(1, 2, 3))


def per_device(
    solution_in,
    residual_in,
    direction_in,
    legendre,
    inverse_prior,
    noise_qq,
    noise_qu,
    noise_uu,
    pixel_mask,
    cycle_phase,
    m_values,
):
    phi_local = noise_qq.shape[1]
    cycles_here = noise_qq.shape[0]
    modes_here = solution_in.shape[1]
    sections = lax.axis_size("sec")
    group_index = lax.axis_index("grp")
    local_phase = lax.dynamic_slice_in_dim(cycle_phase, group_index * cycles_here, cycles_here, 0)
    angle = m_values.astype(jnp.float32)[:, None] * local_phase[None, :]
    cosines = jnp.cos(angle)
    sine_table = jnp.sin(angle)
    local_m = lax.dynamic_slice_in_dim(m_values, group_index * modes_here, modes_here, 0)
    slot_angle = local_m.astype(jnp.float32)[:, None] * cycle_phase[None, :]
    slot_cos = jnp.cos(slot_angle)
    slot_sin = jnp.sin(slot_angle)
    mask_f = pixel_mask.astype(jnp.float32)
    prior = jnp.repeat(inverse_prior, 2, axis=0)[None, None]
    table = phi_table(m_values, lax.axis_index("sec") * phi_local, phi_local, phi_local * sections)
    solution, residual, direction = (solution_in, residual_in, direction_in)
    for step in range(ITERS):
        apply_field = legendre_forward(direction, legendre)
        field = lax.all_to_all(apply_field, "grp", split_axis=3, concat_axis=1, tiled=True)
        field = lax.psum(field, "sec")
        partial_field = pixel_segment(
            field, cosines, sine_table, table, noise_qq, noise_qu, noise_uu, mask_f
        )
        folded = lax.all_to_all(partial_field, "grp", split_axis=1, concat_axis=3, tiled=True)
        folded = lax.psum(folded, "sec")
        mode_field = rotate_back(folded, slot_cos, slot_sin)
        image = prior * direction + legendre_adjoint(mode_field, legendre)
        norm_now, curve, cross, square = lax.psum(
            (
                totals(residual * residual),
                totals(direction * image),
                totals(residual * image),
                totals(image * image),
            ),
            ("sec", "grp"),
        )
        step_size = norm_now / curve
        alpha = step_size[:, None, None, None]
        solution = solution + alpha * direction
        residual = residual - alpha * image
        norm_next = norm_now - 2.0 * step_size * cross + step_size * step_size * square
        direction = residual + (norm_next / norm_now)[:, None, None, None] * direction
    return (solution, residual, direction)


def solution(mesh):
    return jax.shard_map(
        per_device,
        mesh=mesh,
        in_specs=(
            P(None, "grp", None, "sec"),
            P(None, "grp", None, "sec"),
            P(None, "grp", None, "sec"),
            P("grp", None, None, "sec"),
            P(None, "sec"),
            P("grp", "sec"),
            P("grp", "sec"),
            P("grp", "sec"),
            P("grp", "sec"),
            P(),
            P(),
        ),
        out_specs=(
            P(None, "grp", None, "sec"),
            P(None, "grp", None, "sec"),
            P(None, "grp", None, "sec"),
        ),
        check_vma=False,
    )
```

profile of v0, /device:TPU:0, one launch (start us, length us, event | category | flops | bytes accessed | tf_op | source)
XLA Modules:
  0.0 451.1 jit_solution(6203677750327580794)
XLA Ops:
  0.7 1.9 copy-done
  2.5 1.9 fusion.40
  5.5 2.4 reshape.484
  7.9 7.3 %all-to-all-start = ((f32[8,1,512]{2,1,0:T(1,128)}), f32[8,1,512]{2,1,0:T(1,128)S(1)}, u32[]{:S(2)}, u32[]{:S(2)}) async-start(f32[8,1,512]{2,1,0:T(1,128)} %reshape.484), calls=%async_computation | async-start | bytes 32768 | tf_op jit(solution)/shard_map/all_to_all | solution.py:133
  15.5 1.1 cosine_multiply_fusion
  18.3 1.6 convert_element_type.80
  19.8 1.9 all-to-all-done
  22.9 1.6 reshape.485
  24.6 2.2 copy.135
  26.8 12.4 %psum.169 = f32[2,32,2,2,16]{4,1,3,2,0:T(8,128)} all-reduce(f32[2,32,2,2,16]{4,1,3,2,0:T(8,128)} %bitcast.348), channel_id=1, replica_groups=mesh['sec'=4,'grp'=8] {'sec'}, use_global_device_ids=true, to_apply=%region_2.3 | all-reduce | flops 4096 | bytes 32768 | tf_op jit(solution)/shard_map/psum | solution.py:134
  42.5 1.5 fusion.70
  44.1 1.2 add_multiply_fusion.7
  45.3 2.5 fusion.52
  48.6 1.6 reshape.486
  50.2 4.5 all-to-all-start.1
  54.7 1.1 multiply_reduce_fusion.15
  55.8 5.5 %all-to-all-done.1 = f32[8,1,512]{2,1,0:T(1,128)S(1)} async-done(((f32[8,1,512]{2,1,0:T(1,128)}), f32[8,1,512]{2,1,0:T(1,128)S(1)}, u32[]{:S(2)}, u32[]{:S(2)}) %all-to-all-start.1) | async-done | bytes 16416 | tf_op jit(solution)/shard_map/all_to_all | solution.py:138
  65.4 10.1 %psum.170 = f32[2,4,2,2,128]{4,3,2,1,0:T(2,128)S(1)} all-reduce(f32[2,4,2,2,128]{4,3,2,1,0:T(2,128)S(1)} %reshape.451), channel_id=1, replica_groups=mesh['sec'=4,'grp'=8] {'sec'}, use_global_device_ids=true, to_apply=%region_3.4 | all-reduce | flops 4096 | bytes 32768 | tf_op jit(solution)/shard_map/psum | solution.py:139
  75.6 2.2 multiply_reduce_fusion.12
  77.9 38.3 %all-reduce.3 = (f32[2]{0:T(128)S(1)}, f32[2]{0:T(128)S(1)}, f32[2]{0:T(128)S(1)}, f32[2]{0:T(128)S(1)}) all-reduce(f32[2]{0:T(128)S(1)} %multiply_reduce_fusion.15, f32[2]{0:T(128)S(1)} %get-tuple-element.29, f32[2]{0:T(128)S(1)} %get-tuple-element.28, f32[2]{0:T(128)S(1)} %get-tuple-element.27), channel_id=1, replica_groups=mesh['sec'=4,'grp'=8] {'sec','grp'}, use_global_device_ids=true, to_apply=%region_1.2 | all-reduce | flops 8 | bytes 64 | tf_op jit(solution)/shard_map/psum | solution.py:142
  116.2 1.9 multiply_add_fusion.3
  120.9 1.8 reshape.488
  122.7 10.9 %all_to_all.144 = f32[8,1,512]{2,1,0:T(1,128)S(1)} all-to-all(f32[8,1,512]{2,1,0:T(1,128)S(1)} %reshape.488), channel_id=1, replica_groups=mesh['sec'=4,'grp'=8] {'grp'}, dimensions={0} | all-to-all | bytes 32768 | tf_op jit(solution)/shard_map/all_to_all | solution.py:133
  134.3 1.6 reshape.489
  135.9 2.2 copy.153
  138.1 1.6 copy.154
  139.7 12.6 %psum.175 = f32[2,32,2,2,16]{4,1,2,0,3:T(8,128)} all-reduce(f32[2,32,2,2,16]{4,1,2,0,3:T(8,128)} %copy.154), channel_id=1, replica_groups=mesh['sec'=4,'grp'=8] {'sec'}, use_global_device_ids=true, to_apply=%region_12.13 | all-reduce | flops 4096 | bytes 32768 | tf_op jit(solution)/shard_map/psum | solution.py:134
  155.6 1.5 fusion.68
  157.1 1.2 add_multiply_fusion.5
  158.4 2.5 fusion.55
  162.7 8.9 %all_to_all.145 = f32[8,1,512]{2,1,0:T(1,128)S(1)} all-to-all(f32[8,1,512]{2,1,0:T(1,128)S(1)} %reshape.490), channel_id=1, replica_groups=mesh['sec'=4,'grp'=8] {'grp'}, dimensions={0} | all-to-all | bytes 32768 | tf_op jit(solution)/shard_map/all_to_all | solution.py:138
  175.7 10.1 %psum.176 = f32[2,4,2,2,128]{4,3,2,1,0:T(2,128)S(1)} all-reduce(f32[2,4,2,2,128]{4,3,2,1,0:T(2,128)S(1)} %reshape.454), channel_id=1, replica_groups=mesh['sec'=4,'grp'=8] {'sec'}, use_global_device_ids=true, to_apply=%region_13.14 | all-reduce | flops 4096 | bytes 32768 | tf_op jit(solution)/shard_map/psum | solution.py:139
  186.0 2.2 multiply_reduce_fusion.8
  188.2 38.7 %all-reduce.2 = (f32[2]{0:T(128)S(1)}, f32[2]{0:T(128)S(1)}, f32[2]{0:T(128)S(1)}, f32[2]{0:T(128)S(1)}) all-reduce(f32[2]{0:T(128)S(1)} %get-tuple-element.26, f32[2]{0:T(128)S(1)} %get-tuple-element.25, f32[2]{0:T(128)S(1)} %get-tuple-element.24, f32[2]{0:T(128)S(1)} %get-tuple-element.23), channel_id=1, replica_groups=mesh['sec'=4,'grp'=8] {'sec','grp'}, use_global_device_ids=true, to_apply=%region_7.8 | all-reduce | flops 8 | bytes 64 | tf_op jit(solution)/shard_map/psum | solution.py:142
  227.0 1.9 multiply_add_fusion.2
  231.7 1.8 reshape.492
  233.4 10.9 %all_to_all.146 = f32[8,1,512]{2,1,0:T(1,128)S(1)} all-to-all(f32[8,1,512]{2,1,0:T(1,128)S(1)} %reshape.492), channel_id=1, replica_groups=mesh['sec'=4,'grp'=8] {'grp'}, dimensions={0} | all-to-all | bytes 32768 | tf_op jit(solution)/shard_map/all_to_all | solution.py:133
  245.0 1.6 reshape.493
  246.7 2.2 copy.165
  248.9 1.6 copy.166
  250.4 12.4 %psum.181 = f32[2,32,2,2,16]{4,1,2,0,3:T(8,128)} all-reduce(f32[2,32,2,2,16]{4,1,2,0,3:T(8,128)} %copy.166), channel_id=1, replica_groups=mesh['sec'=4,'grp'=8] {'sec'}, use_global_device_ids=true, to_apply=%region_22.23 | all-reduce | flops 4096 | bytes 32768 | tf_op jit(solution)/shard_map/psum | solution.py:134
  266.1 1.5 fusion.66
  267.7 1.2 add_multiply_fusion.3
  268.9 2.5 fusion.58
  273.2 8.9 %all_to_all.147 = f32[8,1,512]{2,1,0:T(1,128)S(1)} all-to-all(f32[8,1,512]{2,1,0:T(1,128)S(1)} %reshape.494), channel_id=1, replica_groups=mesh['sec'=4,'grp'=8] {'grp'}, dimensions={0} | all-to-all | bytes 32768 | tf_op jit(solution)/shard_map/all_to_all | solution.py:138
  286.2 10.1 %psum.182 = f32[2,4,2,2,128]{4,3,2,1,0:T(2,128)S(1)} all-reduce(f32[2,4,2,2,128]{4,3,2,1,0:T(2,128)S(1)} %reshape.457), channel_id=1, replica_groups=mesh['sec'=4,'grp'=8] {'sec'}, use_global_device_ids=true, to_apply=%region_23.24 | all-reduce | flops 4096 | bytes 32768 | tf_op jit(solution)/shard_map/psum | solution.py:139
  296.5 2.2 multiply_reduce_fusion.4
  298.7 38.7 %all-reduce.1 = (f32[2]{0:T(128)S(1)}, f32[2]{0:T(128)S(1)}, f32[2]{0:T(128)S(1)}, f32[2]{0:T(128)S(1)}) all-reduce(f32[2]{0:T(128)S(1)} %get-tuple-element.22, f32[2]{0:T(128)S(1)} %get-tuple-element.21, f32[2]{0:T(128)S(1)} %get-tuple-element.20, f32[2]{0:T(128)S(1)} %get-tuple-element.19), channel_id=1, replica_groups=mesh['sec'=4,'grp'=8] {'sec','grp'}, use_global_device_ids=true, to_apply=%region_17.18 | all-reduce | flops 8 | bytes 64 | tf_op jit(solution)/shard_map/psum | solution.py:142
  337.5 1.9 multiply_add_fusion.1
  341.1 1.0 copy.176
  342.2 1.8 reshape.496
  344.0 10.9 %all_to_all.148 = f32[8,1,512]{2,1,0:T(1,128)S(1)} all-to-all(f32[8,1,512]{2,1,0:T(1,128)S(1)} %reshape.496), channel_id=1, replica_groups=mesh['sec'=4,'grp'=8] {'grp'}, dimensions={0} | all-to-all | bytes 32768 | tf_op jit(solution)/shard_map/all_to_all | solution.py:133
  355.5 1.6 reshape.497
  357.2 2.2 copy.177
  359.4 1.6 copy.178
  361.0 12.4 %psum.187 = f32[2,32,2,2,16]{4,1,2,0,3:T(8,128)} all-reduce(f32[2,32,2,2,16]{4,1,2,0,3:T(8,128)} %copy.178), channel_id=1, replica_groups=mesh['sec'=4,'grp'=8] {'sec'}, use_global_device_ids=true, to_apply=%region_32.33 | all-reduce | flops 4096 | bytes 32768 | tf_op jit(solution)/shard_map/psum | solution.py:134
  376.0 1.5 fusion.64
  377.6 1.2 add_multiply_fusion.1
  378.8 2.5 fusion.61
  383.1 8.9 %all_to_all.149 = f32[8,1,512]{2,1,0:T(1,128)S(1)} all-to-all(f32[8,1,512]{2,1,0:T(1,128)S(1)} %reshape.498), channel_id=1, replica_groups=mesh['sec'=4,'grp'=8] {'grp'}, dimensions={0} | all-to-all | bytes 32768 | tf_op jit(solution)/shard_map/all_to_all | solution.py:138
  396.1 10.1 %psum.188 = f32[2,4,2,2,128]{4,3,2,1,0:T(2,128)S(1)} all-reduce(f32[2,4,2,2,128]{4,3,2,1,0:T(2,128)S(1)} %reshape.460), channel_id=1, replica_groups=mesh['sec'=4,'grp'=8] {'sec'}, use_global_device_ids=true, to_apply=%region_33.34 | all-reduce | flops 4096 | bytes 32768 | tf_op jit(solution)/shard_map/psum | solution.py:139
  406.4 2.2 multiply_reduce_fusion.1
  408.7 38.7 %all-reduce = (f32[2]{0:T(128)S(1)}, f32[2]{0:T(128)S(1)}, f32[2]{0:T(128)S(1)}, f32[2]{0:T(128)S(1)}) all-reduce(f32[2]{0:T(128)S(1)} %get-tuple-element.18, f32[2]{0:T(128)S(1)} %get-tuple-element.17, f32[2]{0:T(128)S(1)} %get-tuple-element.16, f32[2]{0:T(128)S(1)} %get-tuple-element.15), channel_id=1, replica_groups=mesh['sec'=4,'grp'=8] {'sec','grp'}, use_global_device_ids=true, to_apply=%region_27.28 | all-reduce | flops 8 | bytes 64 | tf_op jit(solution)/shard_map/psum | solution.py:142
  447.4 1.6 multiply_add_fusion
  (136 shorter events, 51.0 us)
Async XLA Ops:
  0.6 1.9 copy-start
  0.6 14.5 %copy-start.7 = (s32[32]{0:T(128)S(1)}, s32[32]{0:T(128)}, u32[]{:S(2)}) copy-start(s32[32]{0:T(128)} %param.21) | copy-start | bytes 388
  0.7 14.6 %copy-start.8 = (f32[128]{0:T(128)S(1)}, f32[128]{0:T(128)}, u32[]{:S(2)}) copy-start(f32[128]{0:T(128)} %param.20) | copy-start | bytes 1540
  7.9 13.9 %all-to-all-start = ((f32[8,1,512]{2,1,0:T(1,128)}), f32[8,1,512]{2,1,0:T(1,128)S(1)}, u32[]{:S(2)}, u32[]{:S(2)}) async-start(f32[8,1,512]{2,1,0:T(1,128)} %reshape.484), calls=%async_computation | async-start | bytes 32768 | tf_op jit(solution)/shard_map/all_to_all | solution.py:133
  16.6 0.7 copy-start.1
  24.6 31.2 %copy-start.6 = (f32[2,1536]{1,0:T(2,128)S(1)}, f32[2,1536]{1,0:T(2,128)}, u32[]{:S(2)}) copy-start(f32[2,1536]{1,0:T(2,128)} %param.15) | copy-start | bytes 36868
  50.2 11.1 %all-to-all-start.1 = ((f32[8,1,512]{2,1,0:T(1,128)}), f32[8,1,512]{2,1,0:T(1,128)S(1)}, u32[]{:S(2)}, u32[]{:S(2)}) async-start(f32[8,1,512]{2,1,0:T(1,128)} %reshape.486), calls=%async_computation.1 | async-start | bytes 32768 | tf_op jit(solution)/shard_map/all_to_all | solution.py:138
  118.2 0.7 copy-start.2
  228.9 0.7 copy-start.4
  339.4 0.7 copy-start.5
  378.8 68.6 %copy-start.3 = (f32[2,4,4,1536]{3,2,0,1:T(4,128)S(1)}, f32[2,4,4,1536]{3,2,0,1:T(4,128)}, u32[]{:S(2)}) copy-start(f32[2,4,4,1536]{3,2,0,1:T(4,128)} %copy-done.2) | copy-start | bytes 589828
where the time goes:
time: 454 us; the launch traced here: 451 us
  blocking collectives  304 us (67%)
  local copies, waits for them, and re-layouts  67 us (15%)
  matrix products  29.7 us (7%)
  other arithmetic  29.5 us (6%)
  starting transfers between devices  11.8 us (3%)
  waiting for transfers between devices  7.35 us (2%)
    psum x4, blocking collectives, per_device(): lax.psum((totals(residual * residual), totals(direction * image), totals(...  155 us
    psum x4, blocking collectives, per_device(): field = lax.psum(field, 'sec')  49.9 us
    psum x4, blocking collectives, per_device(): folded = lax.psum(folded, 'sec')  40.5 us
    all_to_all x3, blocking collectives, per_device(): lax.all_to_all(apply_field, 'grp', split_axis=3, concat_axis=1, tiled=True)  32.7 us
    unnamed x37, local copies, waits for them, and re-layouts  28.9 us
    all_to_all x3, blocking collectives, per_device(): lax.all_to_all(partial_field, 'grp', split_axis=1, concat_axis=3, tiled=T...  26.8 us
    dot_general x4, matrix products, pixel_segment(): jnp.dot(weighted, table.T, precision=lax.Precision.HIGHEST, preferred_ele...  9.92 us
    all_to_all x5, local copies, waits for them, and re-layouts, per_device(): lax.all_to_all(apply_field, 'grp', split_axis=3, concat_axis=1, tiled=True)  9.38 us
  transfers between devices with their start and end apart: 2, of which 2 were waited for; matrix products, arithmetic and copies ran while one was open for 1% of the time, Pallas kernels for 0%

commit v1 on v0

--- a/solution.py
+++ b/solution.py
@@ -136,7 +136,9 @@
             field, cosines, sine_table, table, noise_qq, noise_qu, noise_uu, mask_f
         )
         folded = lax.all_to_all(partial_field, "grp", split_axis=1, concat_axis=3, tiled=True)
-        folded = lax.psum(folded, "sec")
+        folded = folded
+        for hop in (1, 2):
+            folded = folded + lax.ppermute(folded, "sec", [(dev, dev ^ hop) for dev in range(4)])
         mode_field = rotate_back(folded, slot_cos, slot_sin)
         image = prior * direction + legendre_adjoint(mode_field, legendre)
         norm_now, curve, cross, square = lax.psum(

time: 454 us -> 433 us (0.954)
  blocking collectives: 304 us -> 264 us
  waiting for transfers between devices: 7.35 us -> 19.4 us
  starting transfers between devices: 11.8 us -> 19.5 us
    psum x4 -> x0, blocking collectives: 40.5 us -> none  [per_device(): folded = lax.psum(folded, 'sec')]
    ppermute x0 -> x8, waiting for transfers between devices: none -> 10.8 us  [per_device(): lax.ppermute(folded, 'sec', [(dev, dev ^ hop) for dev in range(4)])]
    ppermute x0 -> x8, starting transfers between devices: none -> 7.86 us  [per_device(): lax.ppermute(folded, 'sec', [(dev, dev ^ hop) for dev in range(4)])]
    all_to_all x8 -> x12, local copies, waits for them, and re-layouts: 6.35 us -> 10.4 us  [per_device(): lax.all_to_all(partial_field, 'grp', split_axis=1, concat_axis=3, tiled=T...]
  transfers between devices with their start and end apart: 2 -> 10, of which waited for: 2 -> 10; matrix products, arithmetic and copies ran while one was open for 1% -> 1% of each run, Pallas kernels for 0% -> 0%
where the time goes in v1:
time: 433 us; the launch traced here: 430 us
  blocking collectives  264 us (61%)
  local copies, waits for them, and re-layouts  66.9 us (15%)
  matrix products  29.6 us (7%)
  other arithmetic  29.5 us (7%)
  starting transfers between devices  19.5 us (5%)
  waiting for transfers between devices  19.4 us (4%)
    psum x4, blocking collectives, per_device(): lax.psum((totals(residual * residual), totals(direction * image), totals(...  155 us
    psum x4, blocking collectives, per_device(): field = lax.psum(field, 'sec')  49.9 us
    all_to_all x3, blocking collectives, per_device(): lax.all_to_all(apply_field, 'grp', split_axis=3, concat_axis=1, tiled=True)  32.7 us
    unnamed x37, local copies, waits for them, and re-layouts  28.9 us
    all_to_all x3, blocking collectives, per_device(): lax.all_to_all(partial_field, 'grp', split_axis=1, concat_axis=3, tiled=T...  26.8 us
    ppermute x8, waiting for transfers between devices, per_device(): lax.ppermute(folded, 'sec', [(dev, dev ^ hop) for dev in range(4)])  10.8 us
    all_to_all x12, local copies, waits for them, and re-layouts, per_device(): lax.all_to_all(partial_field, 'grp', split_axis=1, concat_axis=3, tiled=T...  10.4 us
    dot_general x4, matrix products, pixel_segment(): jnp.dot(weighted, table.T, precision=lax.Precision.HIGHEST, preferred_ele...  9.88 us
  transfers between devices with their start and end apart: 10, of which 10 were waited for; matrix products, arithmetic and copies ran while one was open for 1% of the time, Pallas kernels for 0%

profile of v1, /device:TPU:0, one launch (start us, length us, event | category | flops | bytes accessed | tf_op | source)
XLA Modules:
  0.0 430.4 jit_solution(11527141634017926927)
XLA Ops:
  0.7 1.9 copy-done
  2.5 1.9 fusion.40
  5.5 2.4 reshape.480
  7.9 7.3 %all-to-all-start = ((f32[8,1,512]{2,1,0:T(1,128)}), f32[8,1,512]{2,1,0:T(1,128)S(1)}, u32[]{:S(2)}, u32[]{:S(2)}) async-start(f32[8,1,512]{2,1,0:T(1,128)} %reshape.480), calls=%async_computation | async-start | bytes 32768 | tf_op jit(solution)/shard_map/all_to_all | solution.py:133
  18.1 1.6 convert_element_type.80
  19.7 2.1 all-to-all-done
  22.9 1.6 reshape.481
  24.6 2.2 copy.135
  26.8 12.4 %psum.141 = f32[2,32,2,2,16]{4,1,3,2,0:T(8,128)} all-reduce(f32[2,32,2,2,16]{4,1,3,2,0:T(8,128)} %bitcast.352), channel_id=1, replica_groups=mesh['sec'=4,'grp'=8] {'sec'}, use_global_device_ids=true, to_apply=%region_2.3 | all-reduce | flops 4096 | bytes 32768 | tf_op jit(solution)/shard_map/psum | solution.py:134
  42.5 1.5 fusion.70
  44.1 1.2 add_multiply_fusion.7
  45.3 2.5 fusion.52
  48.6 1.6 reshape.482
  50.2 4.3 %all-to-all-start.1 = ((f32[8,1,512]{2,1,0:T(1,128)}), f32[8,1,512]{2,1,0:T(1,128)S(1)}, u32[]{:S(2)}, u32[]{:S(2)}) async-start(f32[8,1,512]{2,1,0:T(1,128)} %reshape.482), calls=%async_computation.1 | async-start | bytes 32768 | tf_op jit(solution)/shard_map/all_to_all | solution.py:138
  54.6 6.5 %all-to-all-done.1 = f32[8,1,512]{2,1,0:T(1,128)S(1)} async-done(((f32[8,1,512]{2,1,0:T(1,128)}), f32[8,1,512]{2,1,0:T(1,128)S(1)}, u32[]{:S(2)}, u32[]{:S(2)}) %all-to-all-start.1) | async-done | bytes 16416 | tf_op jit(solution)/shard_map/all_to_all | solution.py:138
  66.4 1.6 collective-permute-start.1
  70.3 2.2 multiply_reduce_fusion.12
  72.6 38.3 %all-reduce.3 = (f32[2]{0:T(128)S(1)}, f32[2]{0:T(128)S(1)}, f32[2]{0:T(128)S(1)}, f32[2]{0:T(128)S(1)}) all-reduce(f32[2]{0:T(128)S(1)} %multiply_reduce_fusion.15, f32[2]{0:T(128)S(1)} %get-tuple-element.29, f32[2]{0:T(128)S(1)} %get-tuple-element.28, f32[2]{0:T(128)S(1)} %get-tuple-element.27), channel_id=1, replica_groups=mesh['sec'=4,'grp'=8] {'sec','grp'}, use_global_device_ids=true, to_apply=%region_1.2 | all-reduce | flops 8 | bytes 64 | tf_op jit(solution)/shard_map/psum | solution.py:144
  111.0 1.9 multiply_add_fusion.3
  115.6 1.8 reshape.484
  117.4 10.9 %all_to_all.144 = f32[8,1,512]{2,1,0:T(1,128)S(1)} all-to-all(f32[8,1,512]{2,1,0:T(1,128)S(1)} %reshape.484), channel_id=1, replica_groups=mesh['sec'=4,'grp'=8] {'grp'}, dimensions={0} | all-to-all | bytes 32768 | tf_op jit(solution)/shard_map/all_to_all | solution.py:133
  129.0 1.6 reshape.485
  130.6 2.2 copy.153
  132.9 1.6 copy.154
  134.4 12.6 %psum.146 = f32[2,32,2,2,16]{4,1,2,0,3:T(8,128)} all-reduce(f32[2,32,2,2,16]{4,1,2,0,3:T(8,128)} %copy.154), channel_id=1, replica_groups=mesh['sec'=4,'grp'=8] {'sec'}, use_global_device_ids=true, to_apply=%region_11.12 | all-reduce | flops 4096 | bytes 32768 | tf_op jit(solution)/shard_map/psum | solution.py:134
  150.3 1.5 fusion.68
  151.8 1.2 add_multiply_fusion.5
  153.1 2.5 fusion.55
  157.4 8.9 %all_to_all.145 = f32[8,1,512]{2,1,0:T(1,128)S(1)} all-to-all(f32[8,1,512]{2,1,0:T(1,128)S(1)} %reshape.486), channel_id=1, replica_groups=mesh['sec'=4,'grp'=8] {'grp'}, dimensions={0} | all-to-all | bytes 32768 | tf_op jit(solution)/shard_map/all_to_all | solution.py:138
  171.7 2.0 collective-permute-start.3
  173.7 1.7 collective-permute-done.3
  175.6 2.2 multiply_reduce_fusion.8
  177.8 38.7 %all-reduce.2 = (f32[2]{0:T(128)S(1)}, f32[2]{0:T(128)S(1)}, f32[2]{0:T(128)S(1)}, f32[2]{0:T(128)S(1)}) all-reduce(f32[2]{0:T(128)S(1)} %get-tuple-element.26, f32[2]{0:T(128)S(1)} %get-tuple-element.25, f32[2]{0:T(128)S(1)} %get-tuple-element.24, f32[2]{0:T(128)S(1)} %get-tuple-element.23), channel_id=1, replica_groups=mesh['sec'=4,'grp'=8] {'sec','grp'}, use_global_device_ids=true, to_apply=%region_6.7 | all-reduce | flops 8 | bytes 64 | tf_op jit(solution)/shard_map/psum | solution.py:144
  216.6 1.9 multiply_add_fusion.2
  221.3 1.8 reshape.488
  223.0 10.9 %all_to_all.146 = f32[8,1,512]{2,1,0:T(1,128)S(1)} all-to-all(f32[8,1,512]{2,1,0:T(1,128)S(1)} %reshape.488), channel_id=1, replica_groups=mesh['sec'=4,'grp'=8] {'grp'}, dimensions={0} | all-to-all | bytes 32768 | tf_op jit(solution)/shard_map/all_to_all | solution.py:133
  234.6 1.6 reshape.489
  236.3 2.2 copy.165
  238.5 1.6 copy.166
  240.0 12.4 %psum.151 = f32[2,32,2,2,16]{4,1,2,0,3:T(8,128)} all-reduce(f32[2,32,2,2,16]{4,1,2,0,3:T(8,128)} %copy.166), channel_id=1, replica_groups=mesh['sec'=4,'grp'=8] {'sec'}, use_global_device_ids=true, to_apply=%region_20.21 | all-reduce | flops 4096 | bytes 32768 | tf_op jit(solution)/shard_map/psum | solution.py:134
  255.7 1.5 fusion.66
  257.3 1.2 add_multiply_fusion.3
  258.5 2.5 fusion.58
  262.8 8.9 %all_to_all.147 = f32[8,1,512]{2,1,0:T(1,128)S(1)} all-to-all(f32[8,1,512]{2,1,0:T(1,128)S(1)} %reshape.490), channel_id=1, replica_groups=mesh['sec'=4,'grp'=8] {'grp'}, dimensions={0} | all-to-all | bytes 32768 | tf_op jit(solution)/shard_map/all_to_all | solution.py:138
  277.1 2.0 collective-permute-start.5
  279.1 1.7 collective-permute-done.5
  281.0 2.2 multiply_reduce_fusion.4
  283.2 38.8 %all-reduce.1 = (f32[2]{0:T(128)S(1)}, f32[2]{0:T(128)S(1)}, f32[2]{0:T(128)S(1)}, f32[2]{0:T(128)S(1)}) all-reduce(f32[2]{0:T(128)S(1)} %get-tuple-element.22, f32[2]{0:T(128)S(1)} %get-tuple-element.21, f32[2]{0:T(128)S(1)} %get-tuple-element.20, f32[2]{0:T(128)S(1)} %get-tuple-element.19), channel_id=1, replica_groups=mesh['sec'=4,'grp'=8] {'sec','grp'}, use_global_device_ids=true, to_apply=%region_15.16 | all-reduce | flops 8 | bytes 64 | tf_op jit(solution)/shard_map/psum | solution.py:144
  322.0 1.9 multiply_add_fusion.1
  326.7 1.8 reshape.492
  328.4 10.9 %all_to_all.148 = f32[8,1,512]{2,1,0:T(1,128)S(1)} all-to-all(f32[8,1,512]{2,1,0:T(1,128)S(1)} %reshape.492), channel_id=1, replica_groups=mesh['sec'=4,'grp'=8] {'grp'}, dimensions={0} | all-to-all | bytes 32768 | tf_op jit(solution)/shard_map/all_to_all | solution.py:133
  340.0 1.6 reshape.493
  341.7 2.2 copy.177
  343.9 1.6 copy.178
  345.4 12.4 %psum.156 = f32[2,32,2,2,16]{4,1,2,0,3:T(8,128)} all-reduce(f32[2,32,2,2,16]{4,1,2,0,3:T(8,128)} %copy.178), channel_id=1, replica_groups=mesh['sec'=4,'grp'=8] {'sec'}, use_global_device_ids=true, to_apply=%region_29.30 | all-reduce | flops 4096 | bytes 32768 | tf_op jit(solution)/shard_map/psum | solution.py:134
  360.5 1.5 fusion.64
  362.0 1.2 add_multiply_fusion.1
  363.3 2.5 fusion.61
  367.6 8.9 %all_to_all.149 = f32[8,1,512]{2,1,0:T(1,128)S(1)} all-to-all(f32[8,1,512]{2,1,0:T(1,128)S(1)} %reshape.494), channel_id=1, replica_groups=mesh['sec'=4,'grp'=8] {'grp'}, dimensions={0} | all-to-all | bytes 32768 | tf_op jit(solution)/shard_map/all_to_all | solution.py:138
  381.8 2.0 collective-permute-start.7
  383.8 1.7 collective-permute-done.7
  385.7 2.2 multiply_reduce_fusion.1
  388.0 38.8 %all-reduce = (f32[2]{0:T(128)S(1)}, f32[2]{0:T(128)S(1)}, f32[2]{0:T(128)S(1)}, f32[2]{0:T(128)S(1)}) all-reduce(f32[2]{0:T(128)S(1)} %get-tuple-element.18, f32[2]{0:T(128)S(1)} %get-tuple-element.17, f32[2]{0:T(128)S(1)} %get-tuple-element.16, f32[2]{0:T(128)S(1)} %get-tuple-element.15), channel_id=1, replica_groups=mesh['sec'=4,'grp'=8] {'sec','grp'}, use_global_device_ids=true, to_apply=%region_24.25 | all-reduce | flops 8 | bytes 64 | tf_op jit(solution)/shard_map/psum | solution.py:144
  426.7 1.6 multiply_add_fusion
  (152 shorter events, 60.1 us)
Async XLA Ops:
  0.6 1.9 copy-start
  0.6 14.5 %copy-start.7 = (s32[32]{0:T(128)S(1)}, s32[32]{0:T(128)}, u32[]{:S(2)}) copy-start(s32[32]{0:T(128)} %param.21) | copy-start | bytes 388
  0.7 14.5 %copy-start.8 = (f32[128]{0:T(128)S(1)}, f32[128]{0:T(128)}, u32[]{:S(2)}) copy-start(f32[128]{0:T(128)} %param.20) | copy-start | bytes 1540
  7.9 13.9 %all-to-all-start = ((f32[8,1,512]{2,1,0:T(1,128)}), f32[8,1,512]{2,1,0:T(1,128)S(1)}, u32[]{:S(2)}, u32[]{:S(2)}) async-start(f32[8,1,512]{2,1,0:T(1,128)} %reshape.480), calls=%async_computation | async-start | bytes 32768 | tf_op jit(solution)/shard_map/all_to_all | solution.py:133
  16.4 0.7 copy-start.1
  40.1 29.0 %copy-start.6 = (f32[2,1536]{1,0:T(2,128)S(1)}, f32[2,1536]{1,0:T(2,128)}, u32[]{:S(2)}) copy-start(f32[2,1536]{1,0:T(2,128)} %param.15) | copy-start | bytes 36868
  50.2 10.9 %all-to-all-start.1 = ((f32[8,1,512]{2,1,0:T(1,128)}), f32[8,1,512]{2,1,0:T(1,128)S(1)}, u32[]{:S(2)}, u32[]{:S(2)}) async-start(f32[8,1,512]{2,1,0:T(1,128)} %reshape.482), calls=%async_computation.1 | async-start | bytes 32768 | tf_op jit(solution)/shard_map/all_to_all | solution.py:138
  65.2 1.2 collective-permute-start
  66.4 3.7 collective-permute-start.1
  112.9 0.7 copy-start.2
  170.4 1.2 collective-permute-start.2
  171.7 3.7 collective-permute-start.3
  218.5 0.7 copy-start.4
  275.8 1.2 collective-permute-start.4
  277.1 3.7 collective-permute-start.5
  323.9 0.7 copy-start.5
  365.7 61.0 %copy-start.3 = (f32[2,4,4,1536]{3,2,0,1:T(4,128)S(1)}, f32[2,4,4,1536]{3,2,0,1:T(4,128)}, u32[]{:S(2)}) copy-start(f32[2,4,4,1536]{3,2,0,1:T(4,128)} %copy-done.2) | copy-start | bytes 589828
  380.6 1.2 collective-permute-start.6
  381.8 3.7 collective-permute-start.7
